TPU v7x, 32 devices: a whole 2x2x4 slice. The times are simulated.
32 devices in a mesh: pole: 2 (over x), row: 8 (over z, y), col: 2 (over core).
Axes of the slice: x: 2, y: 2, z: 4, core: 2. Of those that a mesh axis runs over, the one named last changes fastest.
Arguments:
- ancestor_inverse: float32 [2, 24576, 12288], P(None, ('pole', 'row'), 'col'), parts along dimension 1, may hold values from -6 to 6
- factor_panels: float32 [4, 2, 24576, 128], P(None, None, ('pole', 'col', 'row')), parts along dimension 2, may hold values from -0.0546875 to 0.0546875
- diag_inverse: float32 [8, 2, 128, 128], P('pole'), parts along dimension 0, may hold values from -6 to 6
- coupling: float32 [4, 2, 128, 128], P('pole'), parts along dimension 0, may hold values from -0.5 to 0.5
- block_pattern: int32 [4, 96], replicated, may hold values from 0 to 1, as said below
- tree_order: int32 [4], replicated, may hold values from 0 to 3, each once
Outputs:
- inverse_panels: float32 [4, 2, 24576, 128], P(None, None, ('pole', 'row')), parts along dimension 2
- inverse_diagonal: float32 [8, 2, 128, 128], P('pole'), parts along dimension 0
- inverse_coupling: float32 [4, 2, 128, 128], P('pole'), parts along dimension 0
There are 2 independent parts, one for each index of `pole`. A program takes and returns all parts, laid end to end along the dimension named above; an argument that names none is the same for every part. Nothing has to cross between parts.
Inputs may be any that keep to these rules, and one draw needn't show every extreme that they name: `tree_order`: each supernode number appears once. `block_pattern`: blocks 0 and 48 lie in every supernode's structure.
All inputs are finite; a program needn't handle non-finite values.
Results may differ from a plain program's by a relative error of at most 0.0001.
Values sent between devices are 32-bit elements; how exact they have to be, the bound alone decides.
A program may use at most 192 MiB of HBM per device.

v0:
```python
import jax
import jax.numpy as jnp
from jax import lax
from jax.sharding import PartitionSpec as P


def swapped(block, axis, bit):
    count = lax.axis_size(axis)
    route = []
    for low in range(count):
        high = low | 1 << bit
        if high != low and high < count:
            route += [(low, high), (high, low)]
    return lax.ppermute(block, axis, route)


def matmul(left_side, right_side):
    return jnp.dot(
        left_side, right_side, preferred_element_type=jnp.float32, precision=lax.Precision.HIGHEST
    )


def multiply(left_side, right_side):
    real_part = matmul(left_side[0], right_side[0]) - matmul(left_side[1], right_side[1])
    imag_part = matmul(left_side[0], right_side[1]) + matmul(left_side[1], right_side[0])
    return jnp.stack([real_part, imag_part])


def flipped(matrix):
    return jnp.swapaxes(matrix, 1, 2)


def row_masks(pattern_eff, first_row, row_count, block_rows):
    row_index = first_row + jnp.arange(row_count, dtype=jnp.int32)
    blocks = row_index // block_rows
    onehot = (blocks[:, None] == jnp.arange(pattern_eff.shape[1], dtype=jnp.int32)[None, :]).astype(
        jnp.float32
    )
    return matmul(pattern_eff, onehot.T)


def per_device(ancestor_inverse, factor_panels, diag_inverse, coupling, block_pattern, tree_order):
    grid_row = lax.axis_index("row")
    grid_col = lax.axis_index("col")
    tile_rows = ancestor_inverse.shape[1]
    half_rows = ancestor_inverse.shape[2]
    piece_rows = factor_panels.shape[2]
    block_rows = factor_panels.shape[3]
    super_count = factor_panels.shape[0]
    share_rows = tile_rows // 2
    sorted_pattern = jnp.take(block_pattern, tree_order, axis=0).astype(jnp.float32)
    pattern_eff = jnp.concatenate(
        [sorted_pattern[:2], sorted_pattern[2:] * sorted_pattern[:2]], axis=0
    )
    source_mask = row_masks(
        pattern_eff, grid_col * half_rows + grid_row * piece_rows, piece_rows, block_rows
    )
    target_mask = row_masks(pattern_eff, grid_row * tile_rows, tile_rows, block_rows)
    panels = jnp.take(factor_panels, tree_order, axis=0) * source_mask[:, None, :, None]
    diag_blocks = jnp.take(diag_inverse, tree_order, axis=0)
    columns = []
    products = []
    for tree_slot in range(super_count):
        gathered = lax.all_gather(panels[tree_slot], "row", axis=1, tiled=True)
        columns.append(gathered)
        products.append(lax.psum(multiply(ancestor_inverse, gathered), "col"))
    own_flag = (grid_row * tile_rows // half_rows == grid_col).astype(jnp.float32)
    offset = jnp.clip(grid_row * tile_rows - grid_col * half_rows, 0, half_rows - tile_rows)
    own_windows = jnp.stack(
        [
            lax.dynamic_slice_in_dim(column_set, offset, tile_rows, 1) * own_flag
            for column_set in columns
        ]
    )
    partner_windows = swapped(own_windows, "col", 0)
    tile_windows = own_windows + partner_windows

    def share(matrix):
        return lax.dynamic_slice_in_dim(matrix, grid_col * share_rows, share_rows, 1)

    windows = [share(tile_windows[tree_slot]) for tree_slot in range(super_count)]
    parent_cols = [
        -target_mask[tree_slot][None, :, None] * products[tree_slot] for tree_slot in range(2)
    ]
    child_cols = [
        -target_mask[tree_slot + 2][None, :, None]
        * (products[tree_slot + 2] + multiply(parent_cols[tree_slot], coupling[tree_slot]))
        for tree_slot in range(2)
    ]
    parent_local = [
        multiply(flipped(windows[tree_slot]), share(parent_cols[tree_slot]))
        for tree_slot in range(2)
    ]
    cross_local = [
        multiply(flipped(share(parent_cols[tree_slot])), windows[tree_slot + 2])
        for tree_slot in range(2)
    ]
    child_local = [
        multiply(flipped(windows[tree_slot + 2]), share(child_cols[tree_slot]))
        for tree_slot in range(2)
    ]
    parent_sums = lax.psum(jnp.stack(parent_local), ("row", "col"))
    parent_diag = [diag_blocks[tree_slot] - parent_sums[tree_slot] for tree_slot in range(2)]
    child_totals = lax.psum(jnp.stack(cross_local + child_local), ("row", "col"))
    crosses = [
        -(child_totals[tree_slot] + multiply(parent_diag[tree_slot], coupling[tree_slot]))
        for tree_slot in range(2)
    ]
    child_sums = [child_totals[2 + tree_slot] for tree_slot in range(2)]
    child_diag = [
        diag_blocks[tree_slot + 2]
        - child_sums[tree_slot]
        - multiply(flipped(coupling[tree_slot]), crosses[tree_slot])
        for tree_slot in range(2)
    ]
    all_cols = jnp.stack(parent_cols + child_cols)
    all_diag = jnp.stack(parent_diag + child_diag)
    inverse_panels = jnp.zeros_like(all_cols).at[tree_order].set(all_cols)
    inverse_diagonal = jnp.zeros_like(all_diag).at[tree_order].set(all_diag)
    return (inverse_panels, inverse_diagonal, jnp.stack(crosses))


def solution(mesh):
    return jax.shard_map(
        per_device,
        mesh=mesh,
        in_specs=(
            P(None, ("pole", "row"), "col"),
            P(None, None, ("pole", "col", "row"), None),
            P("pole", None, None, None),
            P("pole", None, None, None),
            P(),
            P(),
        ),
        out_specs=(
            P(None, None, ("pole", "row"), None),
            P("pole", None, None, None),
            P("pole", None, None, None),
        ),
        check_vma=False,
    )
```

profile of v0, /device:TPU:0, one launch (start us, length us, event | category | flops | bytes accessed | tf_op | source)
XLA Modules:
  0.0 873.5 jit_solution(7536772676169645142)
XLA Ops:
  7.2 0.8 compare_and_fusion
  9.3 1.2 gather_fusion
  10.7 2.4 gather_fusion.1
  13.5 2.4 select_multiply_fusion
  15.8 1.7 fusion.222
  19.7 99.5 %all-gather.11.cloned.1.call-done = f32[1,2,6144,128]{3,2,1,0:T(8,128)} async-done(((f32[1,2,768,128]{3,2,1,0:T(8,128)}), f32[1,2,6144,128]{3,2,1,0:T(8,128)}) %all-gather.11.cloned.1.call-update) | async-done | bytes 6291472 | tf_op jit(solution)/shard_map/all_gather | solution.py:64
  119.2 36.1 %fusion.8 = f32[128,1536]{1,0:T(8,128)S(1)} fusion(f32[2,1536,6144]{2,1,0:T(8,128)} %param.6, f32[1,2,6144,128]{3,2,1,0:T(8,128)} %all-gather.11.cloned.1.call-done), kind=kOutput, calls=%fused_computation.13 | convolution fusion | flops 14495514624 | bytes 41680896 | tf_op jit(solution)/shard_map/dot_general | solution.py:18
  155.3 35.0 %fusion.10 = f32[128,1536]{1,0:T(8,128)S(1)} fusion(f32[2,1536,6144]{2,1,0:T(8,128)} %param.6, f32[1,2,6144,128]{3,2,1,0:T(8,128)S(1)} %copy-done.2), kind=kOutput, calls=%fused_computation.15 | convolution fusion | flops 14495514624 | bytes 41680896 | tf_op jit(solution)/shard_map/dot_general | solution.py:18
  190.3 35.3 %fusion.73 = f32[1,1536,128]{1,2,0:T(8,128)S(1)} fusion(f32[128,1536]{1,0:T(8,128)S(1)} %fusion.8, f32[2,1536,6144]{2,1,0:T(8,128)} %param.6, f32[1,2,6144,128]{3,2,1,0:T(8,128)S(1)} %copy-done.2), kind=kOutput, calls=%fused_computation.79 | convolution fusion | flops 14495711232 | bytes 42467328 | tf_op jit(solution)/shard_map/dot_general | solution.py:18
  225.6 35.6 %fusion.67 = f32[1,1536,128]{1,2,0:T(8,128)S(1)} fusion(f32[128,1536]{1,0:T(8,128)S(1)} %fusion.10, f32[2,1536,6144]{2,1,0:T(8,128)} %param.6, f32[1,2,6144,128]{3,2,1,0:T(8,128)S(1)} %copy-done.2), kind=kOutput, calls=%fused_computation.77 | convolution fusion | flops 14495711232 | bytes 42467328 | tf_op jit(solution)/shard_map/dot_general | solution.py:18
  261.3 36.6 %fusion.4 = f32[128,1536]{1,0:T(8,128)S(1)} fusion(f32[2,1536,6144]{2,1,0:T(8,128)} %param.6, f32[1,2,6144,128]{3,2,1,0:T(8,128)} %all-gather.13.cloned.1.call-done), kind=kOutput, calls=%fused_computation.9 | convolution fusion | flops 14495514624 | bytes 41680896 | tf_op jit(solution)/shard_map/dot_general | solution.py:18
  297.9 35.2 %fusion.6 = f32[128,1536]{1,0:T(8,128)S(1)} fusion(f32[2,1536,6144]{2,1,0:T(8,128)} %param.6, f32[1,2,6144,128]{3,2,1,0:T(8,128)S(1)} %copy-done.3), kind=kOutput, calls=%fused_computation.11 | convolution fusion | flops 14495514624 | bytes 41680896 | tf_op jit(solution)/shard_map/dot_general | solution.py:18
  333.0 1.3 pad_maximum_fusion.3
  334.4 35.2 %fusion.85 = f32[1,1536,128]{1,2,0:T(8,128)S(1)} fusion(f32[128,1536]{1,0:T(8,128)S(1)} %fusion.4, f32[2,1536,6144]{2,1,0:T(8,128)} %param.6, f32[1,2,6144,128]{3,2,1,0:T(8,128)S(1)} %copy-done.3), kind=kOutput, calls=%fused_computation.83 | convolution fusion | flops 14495711232 | bytes 42467328 | tf_op jit(solution)/shard_map/dot_general | solution.py:18
  369.6 35.0 %fusion.79 = f32[1,1536,128]{1,2,0:T(8,128)S(1)} fusion(f32[128,1536]{1,0:T(8,128)S(1)} %fusion.6, f32[2,1536,6144]{2,1,0:T(8,128)} %param.6, f32[1,2,6144,128]{3,2,1,0:T(8,128)S(1)} %copy-done.3), kind=kOutput, calls=%fused_computation.81 | convolution fusion | flops 14495711232 | bytes 42467328 | tf_op jit(solution)/shard_map/dot_general | solution.py:18
  404.7 1.3 pad_maximum_fusion.4
  405.9 36.3 %fusion = f32[128,1536]{1,0:T(8,128)S(1)} fusion(f32[2,1536,6144]{2,1,0:T(8,128)} %param.6, f32[1,2,6144,128]{3,2,1,0:T(8,128)} %all-gather.15.cloned.1.call-done), kind=kOutput, calls=%fused_computation.5 | convolution fusion | flops 14495514624 | bytes 41680896 | tf_op jit(solution)/shard_map/dot_general | solution.py:18
  442.3 35.0 %fusion.2 = f32[128,1536]{1,0:T(8,128)S(1)} fusion(f32[2,1536,6144]{2,1,0:T(8,128)} %param.6, f32[1,2,6144,128]{3,2,1,0:T(8,128)S(1)} %copy-done.4), kind=kOutput, calls=%fused_computation.7 | convolution fusion | flops 14495514624 | bytes 41680896 | tf_op jit(solution)/shard_map/dot_general | solution.py:18
  477.3 35.5 %fusion.97 = f32[1,1536,128]{1,2,0:T(8,128)S(1)} fusion(f32[128,1536]{1,0:T(8,128)S(1)} %fusion, f32[2,1536,6144]{2,1,0:T(8,128)} %param.6, f32[1,2,6144,128]{3,2,1,0:T(8,128)S(1)} %copy-done.4), kind=kOutput, calls=%fused_computation.87 | convolution fusion | flops 14495711232 | bytes 42467328 | tf_op jit(solution)/shard_map/dot_general | solution.py:18
  512.8 35.0 %fusion.91 = f32[1,1536,128]{1,2,0:T(8,128)S(1)} fusion(f32[128,1536]{1,0:T(8,128)S(1)} %fusion.2, f32[2,1536,6144]{2,1,0:T(8,128)} %param.6, f32[1,2,6144,128]{3,2,1,0:T(8,128)S(1)} %copy-done.4), kind=kOutput, calls=%fused_computation.85 | convolution fusion | flops 14495711232 | bytes 42467328 | tf_op jit(solution)/shard_map/dot_general | solution.py:18
  547.9 1.2 pad_maximum_fusion.5
  549.1 36.3 %fusion.12 = f32[128,1536]{1,0:T(8,128)S(1)} fusion(f32[2,1536,6144]{2,1,0:T(8,128)} %param.6, f32[1,2,6144,128]{3,2,1,0:T(8,128)} %all-gather.9.cloned.1.call-done), kind=kOutput, calls=%fused_computation.17 | convolution fusion | flops 14495514624 | bytes 41680896 | tf_op jit(solution)/shard_map/dot_general | solution.py:18
  585.4 35.0 %fusion.14 = f32[128,1536]{1,0:T(8,128)S(1)} fusion(f32[2,1536,6144]{2,1,0:T(8,128)} %param.6, f32[1,2,6144,128]{3,2,1,0:T(8,128)S(1)} %copy-done.5), kind=kOutput, calls=%fused_computation.19 | convolution fusion | flops 14495514624 | bytes 41680896 | tf_op jit(solution)/shard_map/dot_general | solution.py:18
  620.5 35.5 %fusion.61 = f32[1,1536,128]{1,2,0:T(8,128)S(1)} fusion(f32[128,1536]{1,0:T(8,128)S(1)} %fusion.12, f32[2,1536,6144]{2,1,0:T(8,128)} %param.6, f32[1,2,6144,128]{3,2,1,0:T(8,128)S(1)} %copy-done.5), kind=kOutput, calls=%fused_computation.75 | convolution fusion | flops 14495711232 | bytes 42467328 | tf_op jit(solution)/shard_map/dot_general | solution.py:18
  655.9 35.0 %fusion.55 = f32[1,1536,128]{1,2,0:T(8,128)S(1)} fusion(f32[128,1536]{1,0:T(8,128)S(1)} %fusion.14, f32[2,1536,6144]{2,1,0:T(8,128)} %param.6, f32[1,2,6144,128]{3,2,1,0:T(8,128)S(1)} %copy-done.5), kind=kOutput, calls=%fused_computation.73 | convolution fusion | flops 14495711232 | bytes 42467328 | tf_op jit(solution)/shard_map/dot_general | solution.py:18
  691.0 1.3 pad_maximum_fusion.2
  692.4 1.6 dynamic-slice_multiply_fusion.2
  694.0 2.2 dynamic-slice_multiply_fusion.1
  696.2 2.3 dynamic-slice_multiply_fusion
  698.5 2.5 dynamic-slice_multiply_fusion.3
  701.1 2.9 pad_maximum_fusion.1
  704.5 1.7 gather_fusion.2
  708.2 1.5 broadcast_select_fusion
  709.7 13.4 %all-reduce.7.cloned.1.call-done = (f32[2,1536,128]{1,2,0:T(8,128)}, f32[2,1536,128]{1,2,0:T(8,128)}, f32[2,1536,128]{1,2,0:T(8,128)}, f32[2,1536,128]{1,2,0:T(8,128)}) async-done(((f32[2,1536,128]{1,2,0:T(8,128)}, f32[2,1536,128]{1,2,0:T(8,128)}, f32[2,1536,128]{1,2,0:T(8,128)}, f32[2,1536,128]{1,2,0:T(8,128)}), (f32[2,1536,128]{1,2,0:T(8,128)}, f32[2,1536,128]{1,2,0:T(8,128)}, f32[2,1536,128]{1,2,0:T(8,128)}, ...) | async-done | bytes 6291472 | tf_op jit(solution)/shard_map/psum | solution.py:66
  723.1 1.7 broadcast_multiply_fusion
  725.3 0.8 fusion.121
  726.2 0.8 fusion.122
  727.0 0.8 fusion.119
  727.9 0.8 fusion.120
  728.8 1.4 fusion.225
  730.2 1.4 fusion.224
  732.7 3.3 fusion.220
  737.4 0.8 fusion.127
  738.2 0.8 fusion.125
  740.9 0.9 fusion.51
  741.8 0.9 fusion.50
  742.7 0.9 fusion.49
  743.7 0.9 fusion.48
  746.2 0.8 fusion.135
  751.4 0.8 fusion.115
  753.0 0.8 fusion.117
  755.7 0.8 fusion.107
  757.3 0.8 fusion.109
  760.0 0.8 pad_maximum_fusion.6
  760.9 4.3 pad_maximum_fusion
  765.2 6.6 copy.33
  771.8 3.2 broadcast_in_dim.45
  775.0 13.3 %scatter_fusion = f32[4,2,1536,128]{3,2,1,0:T(8,128)} fusion(f32[4,2,1536,128]{3,2,1,0:T(8,128)} %broadcast_in_dim.45, s32[4]{0:T(128)S(1)} %copy-done.32, f32[4,2,1536,128]{3,2,1,0:T(8,128)} %copy.33), kind=kCustom, calls=%fused_computation.3 | custom fusion | bytes 18874384 | tf_op jit(solution)/shard_map/scatter | solution.py:118
  788.3 66.6 %all-reduce.5.cloned.1.call-done = (f32[4,2,128,128]{3,2,1,0:T(8,128)}, f32[2,2,128,128]{3,2,1,0:T(8,128)}) async-done(((f32[4,2,128,128]{3,2,1,0:T(8,128)}, f32[2,2,128,128]{3,2,1,0:T(8,128)}), (f32[4,2,128,128]{3,2,1,0:T(8,128)}, f32[2,2,128,128]{3,2,1,0:T(8,128)})) %all-reduce.5.cloned.1.call-update) | async-done | bytes 786448 | tf_op jit(solution)/shard_map/psum | solution.py:104
  854.9 1.1 slice_subtract_fusion.3
  857.7 1.0 fusion.140
  861.9 0.8 pad_maximum_fusion.7
  862.7 0.8 broadcast_in_dim.51
  863.6 2.7 scatter_fusion.1
  (151 shorter events, 27.0 us)
Async XLA Ops:
  7.2 3.5 copy-start
  7.2 112.0 %all-gather.11.cloned.1.call-start = ((), (), s32[]{:S(2)}) async-start(), calls=%async_computation.1 | async-start | bytes 7077888 | tf_op jit(solution)/shard_map/all_gather | solution.py:64
  8.0 5.4 copy-start.33
  8.8 0.5 copy-start.31
  9.3 3.8 copy-start.30
  10.6 2.4 copy-start.34
  10.6 2.4 copy-start.36
  17.6 243.7 %all-gather.13.cloned.1.call-start = ((), (), s32[]{:S(2)}) async-start(), calls=%async_computation.2 | async-start | bytes 7077888 | tf_op jit(solution)/shard_map/all_gather | solution.py:64
  18.3 387.6 %all-gather.15.cloned.1.call-start = ((), (), s32[]{:S(2)}) async-start(), calls=%async_computation.3 | async-start | bytes 7077888 | tf_op jit(solution)/shard_map/all_gather | solution.py:64
  19.1 530.0 %all-gather.9.cloned.1.call-start = ((), (), s32[]{:S(2)}) async-start(), calls=%async_computation | async-start | bytes 7077888 | tf_op jit(solution)/shard_map/all_gather | solution.py:64
  19.7 703.5 %all-reduce.7.cloned.1.call-start = ((), (), s32[]{:S(2)}) async-start(), calls=%async_computation.5 | async-start | bytes 12582912 | tf_op jit(solution)/shard_map/psum | solution.py:66
  119.2 36.1 %copy-start.2 = (f32[1,2,6144,128]{3,2,1,0:T(8,128)S(1)}, f32[1,2,6144,128]{3,2,1,0:T(8,128)}, u32[]{:S(2)}) copy-start(f32[1,2,6144,128]{3,2,1,0:T(8,128)} %all-gather.11.cloned.1.call-done) | copy-start | bytes 18874372
  261.3 36.6 %copy-start.3 = (f32[1,2,6144,128]{3,2,1,0:T(8,128)S(1)}, f32[1,2,6144,128]{3,2,1,0:T(8,128)}, u32[]{:S(2)}) copy-start(f32[1,2,6144,128]{3,2,1,0:T(8,128)} %all-gather.13.cloned.1.call-done) | copy-start | bytes 18874372
  405.9 36.3 %copy-start.4 = (f32[1,2,6144,128]{3,2,1,0:T(8,128)S(1)}, f32[1,2,6144,128]{3,2,1,0:T(8,128)}, u32[]{:S(2)}) copy-start(f32[1,2,6144,128]{3,2,1,0:T(8,128)} %all-gather.15.cloned.1.call-done) | copy-start | bytes 18874372
  549.1 36.3 %copy-start.5 = (f32[1,2,6144,128]{3,2,1,0:T(8,128)S(1)}, f32[1,2,6144,128]{3,2,1,0:T(8,128)}, u32[]{:S(2)}) copy-start(f32[1,2,6144,128]{3,2,1,0:T(8,128)} %all-gather.9.cloned.1.call-done) | copy-start | bytes 18874372
  692.3 162.6 %all-reduce.5.cloned.1.call-start = ((), (), s32[]{:S(2)}) async-start(), calls=%async_computation.4 | async-start | bytes 1572864 | tf_op jit(solution)/shard_map/psum | solution.py:104
  694.0 7.1 copy-start.10
  696.2 4.9 copy-start.12
  698.5 5.5 copy-start.14
  701.1 3.4 copy-start.16
  701.1 5.2 copy-start.35
  701.1 5.2 copy-start.37
  701.1 6.4 copy-start.18
  704.5 27.2 %collective-permute-start = (f32[4,2,1536,128]{3,2,1,0:T(8,128)}, f32[4,2,1536,128]{3,2,1,0:T(8,128)}, u32[]{:S(2)}, u32[]{:S(2)}) collective-permute-start(f32[4,2,1536,128]{3,2,1,0:T(8,128)} %pad_maximum_fusion.1), channel_id=1, source_target_pairs={{0,1},{1,0},{2,3},{3,2},{4,5},{5,4},{6,7},{7,6},{8,9},{9,8},{10,11... | collective-permute-start | bytes 18874376 | tf_op jit(solution)/shard_map/ppermute | solution.py:14
  723.1 1.9 copy-start.19
  725.3 3.4 copy-start.20
  728.8 2.9 copy-start.11
  728.8 2.9 copy-start.13
  728.8 3.5 copy-start.15
  728.8 3.9 copy-start.17
  743.6 1.4 copy-start.23
  743.6 1.9 copy-start.24
  743.6 1.9 copy-start.28
  743.7 1.9 copy-start.29
  746.2 9.5 %copy-start.8 = (f32[2,1536,128]{1,2,0:T(8,128)}, f32[2,1536,128]{1,2,0:T(8,128)S(1)}, u32[]{:S(2)}) copy-start(f32[2,1536,128]{1,2,0:T(8,128)S(1)} %get-tuple-element.36) | copy-start | bytes 4718596
  746.2 11.1 %copy-start.6 = (f32[2,1536,128]{1,2,0:T(8,128)}, f32[2,1536,128]{1,2,0:T(8,128)S(1)}, u32[]{:S(2)}) copy-start(f32[2,1536,128]{1,2,0:T(8,128)S(1)} %get-tuple-element.35) | copy-start | bytes 4718596
  757.3 3.5 copy-start.9
  758.1 2.7 copy-start.7
  771.8 3.2 copy-start.32
  775.0 79.9 %copy-start.21 = (f32[4,2,128,128]{3,2,1,0:T(8,128)S(1)}, f32[4,2,128,128]{3,2,1,0:T(8,128)}, u32[]{:S(2)}) copy-start(f32[4,2,128,128]{3,2,1,0:T(8,128)} %broadcast_select_fusion) | copy-start | bytes 1572868
  788.3 70.4 %copy-start.26 = (f32[2,128,128]{1,2,0:T(8,128)S(1)}, f32[2,128,128]{1,2,0:T(8,128)}, u32[]{:S(2)}) copy-start(f32[2,128,128]{1,2,0:T(8,128)} %get-tuple-element.31) | copy-start | bytes 393220
  854.9 5.0 copy-start.27
  854.9 6.2 copy-start.22
  854.9 6.2 copy-start.25
  859.9 6.4 copy-start.1
Sparse Core Ops, SparseCore 0:
  17.7 101.4 all-gather.10
  121.4 96.8 all-gather.12
  220.5 96.9 all-gather.14
  320.1 96.8 all-gather.8
  692.4 30.6 all-reduce.6
  761.0 93.8 all-reduce.4
where the time goes:
time: 883 us; the launch traced here: 874 us
  matrix products  597 us (68%)
  waiting for transfers between devices  181 us (20%)
  other arithmetic  41.3 us (5%)
  local copies, waits for them, and re-layouts  38.3 us (4%)
  between operations  15.6 us (2%)
    dot_general x66, matrix products, matmul(): jnp.dot(left_side, right_side, preferred_element_type=jnp.float32, precis...  597 us
    all_gather x4, waiting for transfers between devices, per_device(): gathered = lax.all_gather(panels[tree_slot], 'row', axis=1, tiled=True)  99.5 us
    psum x1, waiting for transfers between devices, per_device(): lax.psum(jnp.stack(cross_local + child_local), ('row', 'col'))  66.6 us
  transfers between devices with their start and end apart: 7, of which 3 were waited for; matrix products, arithmetic and copies ran while one was open for 55% of the time, Pallas kernels for 0%

commit v1 on v0

--- a/solution.py
+++ b/solution.py
@@ -101,7 +101,9 @@
     ]
     parent_sums = lax.psum(jnp.stack(parent_local), ("row", "col"))
     parent_diag = [diag_blocks[tree_slot] - parent_sums[tree_slot] for tree_slot in range(2)]
-    child_totals = lax.psum(jnp.stack(cross_local + child_local), ("row", "col"))
+    child_totals = jnp.stack(cross_local + child_local)
+    for name in ("row", "col"):
+        child_totals = lax.psum(child_totals, name)
     crosses = [
         -(child_totals[tree_slot] + multiply(parent_diag[tree_slot], coupling[tree_slot]))
         for tree_slot in range(2)

time: 883 us -> 976 us (1.11)
  waiting for transfers between devices: 181 us -> 262 us
  matrix products: 597 us -> 610 us
    psum x1 -> x3, waiting for transfers between devices: 66.6 us -> 146 us  [the longest x2 93.9 us: per_device(): child_totals = lax.psum(child_totals, name)]
    dot_general x66, matrix products: 597 us -> 610 us  [matmul(): jnp.dot(left_side, right_side, preferred_element_type=jnp.float32, precis...]
  transfers between devices with their start and end apart: 7 -> 9, of which waited for: 3 -> 5; matrix products, arithmetic and copies ran while one was open for 55% -> 51% of each run, Pallas kernels for 0% -> 0%
where the time goes in v1:
time: 976 us; the launch traced here: 967 us
  matrix products  610 us (62%)
  waiting for transfers between devices  262 us (27%)
  other arithmetic  41 us (4%)
  local copies, waits for them, and re-layouts  38.2 us (4%)
  between operations  15.8 us (2%)
    dot_general x66, matrix products, matmul(): jnp.dot(left_side, right_side, preferred_element_type=jnp.float32, precis...  610 us
    all_gather x4, waiting for transfers between devices, per_device(): gathered = lax.all_gather(panels[tree_slot], 'row', axis=1, tiled=True)  99.5 us
    psum x2, waiting for transfers between devices, per_device(): child_totals = lax.psum(child_totals, name)  93.9 us
    psum x1, waiting for transfers between devices, per_device(): parent_sums = lax.psum(jnp.stack(parent_local), ('row', 'col'))  51.7 us
  transfers between devices with their start and end apart: 9, of which 5 were waited for; matrix products, arithmetic and copies ran while one was open for 51% of the time, Pallas kernels for 0%

profile of v1, /device:TPU:0, one launch (start us, length us, event | category | flops | bytes accessed | tf_op | source)
XLA Modules:
  0.0 967.0 jit_solution(15925034017285489864)
XLA Ops:
  9.4 1.2 gather_fusion
  10.7 2.4 gather_fusion.1
  13.5 2.4 select_multiply_fusion
  15.9 1.7 fusion.222
  19.8 99.5 %all-gather.11.cloned.1.call-done = f32[1,2,6144,128]{3,2,1,0:T(8,128)} async-done(((f32[1,2,768,128]{3,2,1,0:T(8,128)}), f32[1,2,6144,128]{3,2,1,0:T(8,128)}) %all-gather.11.cloned.1.call-update) | async-done | bytes 6291472 | tf_op jit(solution)/shard_map/all_gather | solution.py:64
  119.2 36.1 %fusion.8 = f32[128,1536]{1,0:T(8,128)S(1)} fusion(f32[2,1536,6144]{2,1,0:T(8,128)} %param.6, f32[1,2,6144,128]{3,2,1,0:T(8,128)} %all-gather.11.cloned.1.call-done), kind=kOutput, calls=%fused_computation.13 | convolution fusion | flops 14495514624 | bytes 41680896 | tf_op jit(solution)/shard_map/dot_general | solution.py:18
  155.3 35.0 %fusion.10 = f32[128,1536]{1,0:T(8,128)S(1)} fusion(f32[2,1536,6144]{2,1,0:T(8,128)} %param.6, f32[1,2,6144,128]{3,2,1,0:T(8,128)S(1)} %copy-done.2), kind=kOutput, calls=%fused_computation.15 | convolution fusion | flops 14495514624 | bytes 41680896 | tf_op jit(solution)/shard_map/dot_general | solution.py:18
  190.4 35.3 %fusion.73 = f32[1,1536,128]{1,2,0:T(8,128)S(1)} fusion(f32[128,1536]{1,0:T(8,128)S(1)} %fusion.8, f32[2,1536,6144]{2,1,0:T(8,128)} %param.6, f32[1,2,6144,128]{3,2,1,0:T(8,128)S(1)} %copy-done.2), kind=kOutput, calls=%fused_computation.79 | convolution fusion | flops 14495711232 | bytes 42467328 | tf_op jit(solution)/shard_map/dot_general | solution.py:18
  225.7 35.6 %fusion.67 = f32[1,1536,128]{1,2,0:T(8,128)S(1)} fusion(f32[128,1536]{1,0:T(8,128)S(1)} %fusion.10, f32[2,1536,6144]{2,1,0:T(8,128)} %param.6, f32[1,2,6144,128]{3,2,1,0:T(8,128)S(1)} %copy-done.2), kind=kOutput, calls=%fused_computation.77 | convolution fusion | flops 14495711232 | bytes 42467328 | tf_op jit(solution)/shard_map/dot_general | solution.py:18
  261.3 36.5 %fusion.4 = f32[128,1536]{1,0:T(8,128)S(1)} fusion(f32[2,1536,6144]{2,1,0:T(8,128)} %param.6, f32[1,2,6144,128]{3,2,1,0:T(8,128)} %all-gather.13.cloned.1.call-done), kind=kOutput, calls=%fused_computation.9 | convolution fusion | flops 14495514624 | bytes 41680896 | tf_op jit(solution)/shard_map/dot_general | solution.py:18
  297.9 35.2 %fusion.6 = f32[128,1536]{1,0:T(8,128)S(1)} fusion(f32[2,1536,6144]{2,1,0:T(8,128)} %param.6, f32[1,2,6144,128]{3,2,1,0:T(8,128)S(1)} %copy-done.3), kind=kOutput, calls=%fused_computation.11 | convolution fusion | flops 14495514624 | bytes 41680896 | tf_op jit(solution)/shard_map/dot_general | solution.py:18
  333.1 1.3 pad_maximum_fusion.3
  334.4 35.2 %fusion.85 = f32[1,1536,128]{1,2,0:T(8,128)S(1)} fusion(f32[128,1536]{1,0:T(8,128)S(1)} %fusion.4, f32[2,1536,6144]{2,1,0:T(8,128)} %param.6, f32[1,2,6144,128]{3,2,1,0:T(8,128)S(1)} %copy-done.3), kind=kOutput, calls=%fused_computation.83 | convolution fusion | flops 14495711232 | bytes 42467328 | tf_op jit(solution)/shard_map/dot_general | solution.py:18
  369.6 35.1 %fusion.79 = f32[1,1536,128]{1,2,0:T(8,128)S(1)} fusion(f32[128,1536]{1,0:T(8,128)S(1)} %fusion.6, f32[2,1536,6144]{2,1,0:T(8,128)} %param.6, f32[1,2,6144,128]{3,2,1,0:T(8,128)S(1)} %copy-done.3), kind=kOutput, calls=%fused_computation.81 | convolution fusion | flops 14495711232 | bytes 42467328 | tf_op jit(solution)/shard_map/dot_general | solution.py:18
  404.6 1.3 pad_maximum_fusion.4
  405.9 36.3 %fusion = f32[128,1536]{1,0:T(8,128)S(1)} fusion(f32[2,1536,6144]{2,1,0:T(8,128)} %param.6, f32[1,2,6144,128]{3,2,1,0:T(8,128)} %all-gather.15.cloned.1.call-done), kind=kOutput, calls=%fused_computation.5 | convolution fusion | flops 14495514624 | bytes 41680896 | tf_op jit(solution)/shard_map/dot_general | solution.py:18
  442.2 35.0 %fusion.2 = f32[128,1536]{1,0:T(8,128)S(1)} fusion(f32[2,1536,6144]{2,1,0:T(8,128)} %param.6, f32[1,2,6144,128]{3,2,1,0:T(8,128)S(1)} %copy-done.4), kind=kOutput, calls=%fused_computation.7 | convolution fusion | flops 14495514624 | bytes 41680896 | tf_op jit(solution)/shard_map/dot_general | solution.py:18
  477.3 35.5 %fusion.97 = f32[1,1536,128]{1,2,0:T(8,128)S(1)} fusion(f32[128,1536]{1,0:T(8,128)S(1)} %fusion, f32[2,1536,6144]{2,1,0:T(8,128)} %param.6, f32[1,2,6144,128]{3,2,1,0:T(8,128)S(1)} %copy-done.4), kind=kOutput, calls=%fused_computation.87 | convolution fusion | flops 14495711232 | bytes 42467328 | tf_op jit(solution)/shard_map/dot_general | solution.py:18
  512.7 35.0 %fusion.91 = f32[1,1536,128]{1,2,0:T(8,128)S(1)} fusion(f32[128,1536]{1,0:T(8,128)S(1)} %fusion.2, f32[2,1536,6144]{2,1,0:T(8,128)} %param.6, f32[1,2,6144,128]{3,2,1,0:T(8,128)S(1)} %copy-done.4), kind=kOutput, calls=%fused_computation.85 | convolution fusion | flops 14495711232 | bytes 42467328 | tf_op jit(solution)/shard_map/dot_general | solution.py:18
  547.8 1.3 pad_maximum_fusion.5
  549.0 36.3 %fusion.12 = f32[128,1536]{1,0:T(8,128)S(1)} fusion(f32[2,1536,6144]{2,1,0:T(8,128)} %param.6, f32[1,2,6144,128]{3,2,1,0:T(8,128)} %all-gather.9.cloned.1.call-done), kind=kOutput, calls=%fused_computation.17 | convolution fusion | flops 14495514624 | bytes 41680896 | tf_op jit(solution)/shard_map/dot_general | solution.py:18
  585.3 35.0 %fusion.14 = f32[128,1536]{1,0:T(8,128)S(1)} fusion(f32[2,1536,6144]{2,1,0:T(8,128)} %param.6, f32[1,2,6144,128]{3,2,1,0:T(8,128)S(1)} %copy-done.5), kind=kOutput, calls=%fused_computation.19 | convolution fusion | flops 14495514624 | bytes 41680896 | tf_op jit(solution)/shard_map/dot_general | solution.py:18
  620.4 35.5 %fusion.61 = f32[1,1536,128]{1,2,0:T(8,128)S(1)} fusion(f32[128,1536]{1,0:T(8,128)S(1)} %fusion.12, f32[2,1536,6144]{2,1,0:T(8,128)} %param.6, f32[1,2,6144,128]{3,2,1,0:T(8,128)S(1)} %copy-done.5), kind=kOutput, calls=%fused_computation.75 | convolution fusion | flops 14495711232 | bytes 42467328 | tf_op jit(solution)/shard_map/dot_general | solution.py:18
  655.9 35.0 %fusion.55 = f32[1,1536,128]{1,2,0:T(8,128)S(1)} fusion(f32[128,1536]{1,0:T(8,128)S(1)} %fusion.14, f32[2,1536,6144]{2,1,0:T(8,128)} %param.6, f32[1,2,6144,128]{3,2,1,0:T(8,128)S(1)} %copy-done.5), kind=kOutput, calls=%fused_computation.73 | convolution fusion | flops 14495711232 | bytes 42467328 | tf_op jit(solution)/shard_map/dot_general | solution.py:18
  690.9 1.3 pad_maximum_fusion.2
  692.3 1.6 dynamic-slice_multiply_fusion.2
  693.9 2.2 dynamic-slice_multiply_fusion.1
  696.1 2.3 dynamic-slice_multiply_fusion
  698.4 2.5 dynamic-slice_multiply_fusion.3
  701.0 2.9 pad_maximum_fusion.1
  704.3 1.7 gather_fusion.2
  708.4 14.6 %all-reduce.12.cloned.1.call-done = (f32[2,1536,128]{1,2,0:T(8,128)}, f32[2,1536,128]{1,2,0:T(8,128)}, f32[2,1536,128]{1,2,0:T(8,128)}, f32[2,1536,128]{1,2,0:T(8,128)}) async-done(((f32[2,1536,128]{1,2,0:T(8,128)}, f32[2,1536,128]{1,2,0:T(8,128)}, f32[2,1536,128]{1,2,0:T(8,128)}, f32[2,1536,128]{1,2,0:T(8,128)}), (f32[2,1536,128]{1,2,0:T(8,128)}, f32[2,1536,128]{1,2,0:T(8,128)}, f32[2,1536,128]{1,2,0:T(8,128)}, ...) | async-done | bytes 6291472 | tf_op jit(solution)/shard_map/psum | solution.py:66
  723.0 1.7 broadcast_multiply_fusion
  728.7 1.4 fusion.225
  730.1 1.4 fusion.224
  732.7 3.3 fusion.220
  740.3 1.1 fusion.132
  743.3 0.9 fusion.49
  744.2 0.9 fusion.48
  746.8 1.6 fusion.135
  748.4 1.4 fusion.136
  749.8 1.4 fusion.133
  751.2 1.6 fusion.134
  753.4 1.1 fusion.130
  758.6 1.8 fusion.110
  760.4 1.6 fusion.111
  762.1 1.9 fusion.106
  764.0 1.8 fusion.107
  765.8 1.8 fusion.108
  770.9 2.9 pad_maximum_fusion
  773.8 6.6 copy.33
  780.4 3.2 broadcast_in_dim.45
  783.6 13.1 %scatter_fusion = f32[4,2,1536,128]{3,2,1,0:T(8,128)} fusion(f32[4,2,1536,128]{3,2,1,0:T(8,128)} %broadcast_in_dim.45, s32[4]{0:T(128)S(1)} %copy-done.49, f32[4,2,1536,128]{3,2,1,0:T(8,128)} %copy.33), kind=kCustom, calls=%fused_computation.3 | custom fusion | bytes 18874384 | tf_op jit(solution)/shard_map/scatter | solution.py:120
  797.9 51.7 %all-reduce.6.cloned.1.call-done = f32[2,2,128,128]{3,2,1,0:T(8,128)} async-done(((f32[2,2,128,128]{3,2,1,0:T(8,128)}), f32[2,2,128,128]{3,2,1,0:T(8,128)}) %all-reduce.6.cloned.1.call-update) | async-done | bytes 262160 | tf_op jit(solution)/shard_map/psum | solution.py:102
  849.6 1.0 slice_subtract_fusion.3
  851.6 74.5 %all-reduce.8.cloned.1.call-done = f32[4,2,128,128]{3,2,1,0:T(8,128)} async-done(((f32[4,2,128,128]{3,2,1,0:T(8,128)}), f32[4,2,128,128]{3,2,1,0:T(8,128)}) %all-reduce.8.cloned.1.call-update) | async-done | bytes 524304 | tf_op jit(solution)/shard_map/psum | solution.py:106
  926.8 19.5 %all-reduce.10.cloned.1.call-done = f32[4,2,128,128]{3,2,1,0:T(8,128)} async-done(((f32[4,2,128,128]{3,2,1,0:T(8,128)}), f32[4,2,128,128]{3,2,1,0:T(8,128)}) %all-reduce.10.cloned.1.call-update) | async-done | bytes 524304 | tf_op jit(solution)/shard_map/psum | solution.py:106
  946.3 1.0 fusion.140
  948.6 1.3 fusion.104
  949.9 1.1 fusion.105
  951.0 1.1 fusion.102
  952.1 1.1 fusion.103
  953.3 1.4 fusion.142
  957.0 2.7 scatter_fusion.1
  (193 shorter events, 34.3 us)
Async XLA Ops:
  7.2 3.6 copy-start
  7.2 112.1 %all-gather.11.cloned.1.call-start = ((), (), s32[]{:S(2)}) async-start(), calls=%async_computation.4 | async-start | bytes 7077888 | tf_op jit(solution)/shard_map/all_gather | solution.py:64
  8.0 5.5 copy-start.50
  9.4 3.8 copy-start.47
  10.7 2.4 copy-start.52
  10.7 2.4 copy-start.54
  17.7 243.7 %all-gather.13.cloned.1.call-start = ((), (), s32[]{:S(2)}) async-start(), calls=%async_computation.5 | async-start | bytes 7077888 | tf_op jit(solution)/shard_map/all_gather | solution.py:64
  18.4 387.5 %all-gather.15.cloned.1.call-start = ((), (), s32[]{:S(2)}) async-start(), calls=%async_computation.6 | async-start | bytes 7077888 | tf_op jit(solution)/shard_map/all_gather | solution.py:64
  19.1 529.9 %all-gather.9.cloned.1.call-start = ((), (), s32[]{:S(2)}) async-start(), calls=%async_computation.3 | async-start | bytes 7077888 | tf_op jit(solution)/shard_map/all_gather | solution.py:64
  19.7 703.3 %all-reduce.12.cloned.1.call-start = ((), (), s32[]{:S(2)}) async-start(), calls=%async_computation.7 | async-start | bytes 12582912 | tf_op jit(solution)/shard_map/psum | solution.py:66
  119.2 36.1 %copy-start.2 = (f32[1,2,6144,128]{3,2,1,0:T(8,128)S(1)}, f32[1,2,6144,128]{3,2,1,0:T(8,128)}, u32[]{:S(2)}) copy-start(f32[1,2,6144,128]{3,2,1,0:T(8,128)} %all-gather.11.cloned.1.call-done) | copy-start | bytes 18874372
  261.3 36.6 %copy-start.3 = (f32[1,2,6144,128]{3,2,1,0:T(8,128)S(1)}, f32[1,2,6144,128]{3,2,1,0:T(8,128)}, u32[]{:S(2)}) copy-start(f32[1,2,6144,128]{3,2,1,0:T(8,128)} %all-gather.13.cloned.1.call-done) | copy-start | bytes 18874372
  405.9 36.3 %copy-start.4 = (f32[1,2,6144,128]{3,2,1,0:T(8,128)S(1)}, f32[1,2,6144,128]{3,2,1,0:T(8,128)}, u32[]{:S(2)}) copy-start(f32[1,2,6144,128]{3,2,1,0:T(8,128)} %all-gather.15.cloned.1.call-done) | copy-start | bytes 18874372
  549.0 36.3 %copy-start.5 = (f32[1,2,6144,128]{3,2,1,0:T(8,128)S(1)}, f32[1,2,6144,128]{3,2,1,0:T(8,128)}, u32[]{:S(2)}) copy-start(f32[1,2,6144,128]{3,2,1,0:T(8,128)} %all-gather.9.cloned.1.call-done) | copy-start | bytes 18874372
  692.2 157.4 %all-reduce.6.cloned.1.call-start = ((), (), s32[]{:S(2)}) async-start(), calls=%async_computation | async-start | bytes 524288 | tf_op jit(solution)/shard_map/psum | solution.py:102
  693.9 7.1 copy-start.10
  696.0 4.9 copy-start.12
  698.4 5.5 copy-start.14
  700.9 3.4 copy-start.16
  701.0 5.2 copy-start.53
  701.0 5.2 copy-start.55
  701.0 5.8 copy-start.27
  701.0 6.5 copy-start.51
  704.3 27.2 %collective-permute-start = (f32[4,2,1536,128]{3,2,1,0:T(8,128)}, f32[4,2,1536,128]{3,2,1,0:T(8,128)}, u32[]{:S(2)}, u32[]{:S(2)}) collective-permute-start(f32[4,2,1536,128]{3,2,1,0:T(8,128)} %pad_maximum_fusion.1), channel_id=1, source_target_pairs={{0,1},{1,0},{2,3},{3,2},{4,5},{5,4},{6,7},{7,6},{8,9},{9,8},{10,11... | collective-permute-start | bytes 18874376 | tf_op jit(solution)/shard_map/ppermute | solution.py:14
  723.0 1.9 copy-start.30
  725.2 15.1 %copy-start.23 = (f32[2,128,768]{2,1,0:T(8,128)}, f32[2,128,768]{2,1,0:T(8,128)S(1)}, u32[]{:S(2)}) copy-start(f32[2,128,768]{2,1,0:T(8,128)S(1)} %get-tuple-element.39) | copy-start | bytes 2359300
  725.2 28.1 %copy-start.21 = (f32[2,128,768]{2,1,0:T(8,128)}, f32[2,128,768]{2,1,0:T(8,128)S(1)}, u32[]{:S(2)}) copy-start(f32[2,128,768]{2,1,0:T(8,128)S(1)} %get-tuple-element.40) | copy-start | bytes 2359300
  725.2 3.4 copy-start.31
  728.7 2.8 copy-start.11
  728.7 2.8 copy-start.13
  728.7 3.5 copy-start.15
  728.7 3.9 copy-start.17
  736.4 8.7 copy-start.20
  736.4 16.9 %copy-start.18 = (f32[1,2,1536,128]{3,2,1,0:T(8,128)}, f32[1,2,1536,128]{3,2,1,0:T(8,128)S(1)}, u32[]{:S(2)}) copy-start(f32[1,2,1536,128]{3,2,1,0:T(8,128)S(1)} %get-tuple-element.13) | copy-start | bytes 4718596
  744.2 1.4 copy-start.35
  744.2 1.9 copy-start.36
  745.3 3.1 copy-start.26
  745.3 6.0 copy-start.24
  746.7 9.4 copy-start.6
  746.8 9.4 copy-start.8
  756.9 8.9 copy-start.7
  757.7 4.3 copy-start.9
  758.5 167.6 %all-reduce.8.cloned.1.call-start = ((), (), s32[]{:S(2)}) async-start(), calls=%async_computation.1 | async-start | bytes 1048576 | tf_op jit(solution)/shard_map/psum | solution.py:106
  758.6 9.1 copy-start.25
  758.6 9.1 copy-start.45
  758.6 9.9 %copy-start.19 = (f32[1,2,1536,128]{3,2,1,0:T(8,128)S(1)}, f32[1,2,1536,128]{3,2,1,0:T(8,128)}, u32[]{:S(2)}) copy-start(f32[1,2,1536,128]{3,2,1,0:T(8,128)} %copy-done.18) | copy-start | bytes 4718596
  758.6 9.9 %copy-start.22 = (f32[2,128,768]{2,1,0:T(8,128)S(1)}, f32[2,128,768]{2,1,0:T(8,128)}, u32[]{:S(2)}) copy-start(f32[2,128,768]{2,1,0:T(8,128)} %copy-done.21) | copy-start | bytes 2359300
  758.6 10.4 %copy-start.46 = (f32[128,128]{1,0:T(8,128)S(1)}, f32[128,128]{1,0:T(8,128)}, u32[]{:S(2)}) copy-start(f32[128,128]{1,0:T(8,128)} %fusion.130) | copy-start | bytes 196612
  762.1 8.8 copy-start.28
  762.1 8.8 copy-start.29
  780.4 3.2 copy-start.49
  783.6 13.1 %copy-start.43 = (f32[1,2,128,128]{3,2,1,0:T(8,128)S(1)}, f32[1,2,128,128]{3,2,1,0:T(8,128)}, u32[]{:S(2)}) copy-start(f32[1,2,128,128]{3,2,1,0:T(8,128)} %maximum_bitcast_fusion.5) | copy-start | bytes 393220
  783.6 13.1 %copy-start.44 = (f32[1,2,128,128]{3,2,1,0:T(8,128)S(1)}, f32[1,2,128,128]{3,2,1,0:T(8,128)}, u32[]{:S(2)}) copy-start(f32[1,2,128,128]{3,2,1,0:T(8,128)} %maximum_bitcast_fusion.4) | copy-start | bytes 393220
  783.6 65.9 %copy-start.32 = (f32[4,2,128,128]{3,2,1,0:T(8,128)S(1)}, f32[4,2,128,128]{3,2,1,0:T(8,128)}, u32[]{:S(2)}) copy-start(f32[4,2,128,128]{3,2,1,0:T(8,128)} %broadcast_select_fusion) | copy-start | bytes 1572868
  796.7 150.6 %copy-start.38 = (f32[2,128,128]{1,2,0:T(8,128)S(1)}, f32[2,128,128]{1,2,0:T(8,128)}, u32[]{:S(2)}) copy-start(f32[2,128,128]{1,2,0:T(8,128)} %get-tuple-element.29) | copy-start | bytes 393220
  796.7 151.3 %copy-start.37 = (f32[2,128,128]{1,2,0:T(8,128)S(1)}, f32[2,128,128]{1,2,0:T(8,128)}, u32[]{:S(2)}) copy-start(f32[2,128,128]{1,2,0:T(8,128)} %get-tuple-element.30) | copy-start | bytes 393220
  797.6 148.7 %all-reduce.10.cloned.1.call-start = ((), (), s32[]{:S(2)}) async-start(), calls=%async_computation.2 | async-start | bytes 1048576 | tf_op jit(solution)/shard_map/psum | solution.py:106
  850.6 76.2 %copy-start.33 = (f32[1,2,128,128]{3,2,1,0:T(8,128)}, f32[1,2,128,128]{3,2,1,0:T(8,128)S(1)}, u32[]{:S(2)}) copy-start(f32[1,2,128,128]{3,2,1,0:T(8,128)S(1)} %get-tuple-element.22) | copy-start | bytes 393220
  851.4 96.5 %copy-start.39 = (f32[128,128]{1,0:T(8,128)}, f32[128,128]{1,0:T(8,128)S(1)}, u32[]{:S(2)}) copy-start(f32[128,128]{1,0:T(8,128)S(1)} %convolution_add_fusion.5) | copy-start | bytes 196612
  851.6 96.3 %copy-start.40 = (f32[128,128]{1,0:T(8,128)}, f32[128,128]{1,0:T(8,128)S(1)}, u32[]{:S(2)}) copy-start(f32[128,128]{1,0:T(8,128)S(1)} %convolution_subtract_fusion.5) | copy-start | bytes 196612
  926.6 21.4 %copy-start.41 = (f32[128,128]{1,0:T(8,128)}, f32[128,128]{1,0:T(8,128)S(1)}, u32[]{:S(2)}) copy-start(f32[128,128]{1,0:T(8,128)S(1)} %convolution_add_fusion.3) | copy-start | bytes 196612
  926.8 21.5 %copy-start.42 = (f32[128,128]{1,0:T(8,128)}, f32[128,128]{1,0:T(8,128)S(1)}, u32[]{:S(2)}) copy-start(f32[128,128]{1,0:T(8,128)S(1)} %convolution_subtract_fusion.3) | copy-start | bytes 196612
  946.3 9.1 copy-start.34
  948.6 11.2 %copy-start.1 = (f32[4,2,768,128]{3,2,1,0:T(8,128)S(1)}, f32[4,2,768,128]{3,2,1,0:T(8,128)}, u32[]{:S(2)}) copy-start(f32[4,2,768,128]{3,2,1,0:T(8,128)} %param.7) | copy-start | bytes 9437188
  (1 other events, 0.6 us)
Sparse Core Ops, SparseCore 0:
  17.8 101.4 all-gather.10
  121.4 96.8 all-gather.12
  220.5 96.9 all-gather.14
  320.1 96.8 all-gather.8
  692.3 30.6 all-reduce.11
  758.7 90.8 all-reduce.5
  853.0 73.1 all-reduce.7
  928.5 17.7 all-reduce.9
